TPU v7x, 32 devices: a whole 2x2x4 slice. The times are simulated.
32 devices in a mesh: section: 4 (over y, x), tok: 4 (over z), head: 2 (over core).
Axes of the slice: x: 2, y: 2, z: 4, core: 2. Of those that a mesh axis runs over, the one named last changes fastest.
Arguments:
- group_in: bfloat16 [4, 512, 2048], P('section', 'tok'), may hold values from -6 to 6
- w_qkv: bfloat16 [4, 3, 2048, 2048], P('section', None, 'tok', 'head'), may hold values from -0.125 to 0.125
- w_out: bfloat16 [4, 2048, 2048], P('section', 'head', 'tok'), may hold values from -0.125 to 0.125
- step_sizes: float32 [4, 512, 4], P('section', 'tok', 'head'), may hold values from 0.05 to 1
- fast_weights: bfloat16 [4, 4, 3, 512, 512], P('section', 'head'), may hold values from -0.25 to 0.25
- momentum: bfloat16 [4, 4, 3, 512, 512], P('section', 'head'), may hold values from -16 to 16
- momentum_decay: float32 [4, 4], P('section', 'head'), may hold values from 0.5 to 0.95
- fast_rate: float32 [4, 4], P('section', 'head'), may hold values from 0.3 to 1
Outputs:
- handed: bfloat16 [4, 512, 2048], P('section', 'tok', 'head')
- fast_next: bfloat16 [4, 4, 3, 512, 512], P('section', 'head')
All inputs are finite; a program needn't handle non-finite values.
Results may differ from a plain program's by a relative error of at most 0.015.
Values may be sent and summed in bfloat16 or wider, within the bound.
A program may use at most 128 MiB of HBM per device.

v0:
```python
import jax
import jax.numpy as jnp
from jax import lax
from jax.sharding import PartitionSpec as P

NS_ITERS = 2


coef_linear = 3.4445
coef_cubic = -4.775
coef_quintic = 2.0315


def passed_along(value, axis, steps):
    count = lax.axis_size(axis)
    pairs = [(source, (source + steps) % count) for source in range(count)]
    return lax.ppermute(value, axis, pairs)


def rms_rows(values_in, epsilon):
    return values_in * lax.rsqrt(jnp.mean(values_in * values_in, axis=-1, keepdims=True) + epsilon)


def fast_grads(key_rows, value_rows, step_rates, weights):
    gate_pre = jnp.einsum(
        "thi,hij->thj", key_rows, weights[:, 0], preferred_element_type=jnp.float32
    )
    up_pre = jnp.einsum("thi,hij->thj", key_rows, weights[:, 1], preferred_element_type=jnp.float32)
    squash = jax.nn.sigmoid(gate_pre)
    hidden = (gate_pre * squash * up_pre).astype(jnp.bfloat16)
    errors = (-(step_rates[:, :, None] * value_rows.astype(jnp.float32))).astype(jnp.bfloat16)
    back_hidden = jnp.einsum(
        "thi,hij->thj", errors, weights[:, 2], preferred_element_type=jnp.float32
    )
    grad_gate = (back_hidden * up_pre * squash * (1.0 + gate_pre * (1.0 - squash))).astype(
        jnp.bfloat16
    )
    grad_up = (back_hidden * gate_pre * squash).astype(jnp.bfloat16)
    grad_first = jnp.einsum("thi,thj->hij", key_rows, grad_gate, preferred_element_type=jnp.float32)
    grad_third = jnp.einsum("thi,thj->hij", key_rows, grad_up, preferred_element_type=jnp.float32)
    grad_second = jnp.einsum("thi,thj->hij", errors, hidden, preferred_element_type=jnp.float32)
    return jnp.stack([grad_first, grad_third, grad_second], axis=1)


def newton_step(rows_in, gathered):
    gram_matrix = jnp.einsum(
        "mij,mik->mjk", gathered, gathered, preferred_element_type=jnp.float32
    ).astype(jnp.bfloat16)
    cubic_term = jnp.einsum(
        "mij,mjk->mik", rows_in, gram_matrix, preferred_element_type=jnp.float32
    )
    quintic_term = jnp.einsum(
        "mij,mjk->mik",
        cubic_term.astype(jnp.bfloat16),
        gram_matrix,
        preferred_element_type=jnp.float32,
    )
    return (
        coef_linear * rows_in.astype(jnp.float32)
        + coef_cubic * cubic_term
        + coef_quintic * quintic_term
    ).astype(jnp.bfloat16)


def apply_fast(queries, updated):
    gate_pre = jnp.einsum(
        "thi,hij->thj", queries, updated[:, 0], preferred_element_type=jnp.float32
    )
    up_pre = jnp.einsum("thi,hij->thj", queries, updated[:, 1], preferred_element_type=jnp.float32)
    hidden = (jax.nn.silu(gate_pre) * up_pre).astype(jnp.bfloat16)
    output = jnp.einsum("thj,hij->thi", hidden, updated[:, 2], preferred_element_type=jnp.float32)
    return rms_rows(output, 1e-05).astype(jnp.bfloat16)


def shards(group_in, w_qkv, w_out, step_sizes, fast_weights, momentum, momentum_decay, fast_rate):
    tokens = group_in[0]
    tok_rows = tokens.shape[0]
    local_heads = fast_weights.shape[1]
    fan_width = fast_weights.shape[3]
    hid_width = fast_weights.shape[4]
    half_width = w_qkv.shape[3]
    projected = jnp.einsum(
        "td,jde->jte",
        tokens,
        lax.all_gather(w_qkv[0], "tok", axis=1, tiled=True),
        preferred_element_type=jnp.float32,
    )
    shaped = projected.reshape(3, tok_rows, local_heads, fan_width)
    queries = rms_rows(shaped[0], 1e-06).astype(jnp.bfloat16)
    key_rows = rms_rows(shaped[1], 1e-06).astype(jnp.bfloat16)
    value_rows = shaped[2].astype(jnp.bfloat16)
    gradients = fast_grads(key_rows, value_rows, step_sizes[0], fast_weights[0])
    decay_rate = momentum_decay[0][:, None, None, None]
    summed = lax.psum(gradients.astype(jnp.bfloat16), "tok").astype(jnp.float32)
    moment = decay_rate * momentum[0].astype(jnp.float32) + summed
    norm_values = jnp.sqrt(jnp.sum(moment * moment, axis=(2, 3), keepdims=True))
    iterate = (moment / (norm_values + 1e-06)).astype(jnp.bfloat16)
    iterate = iterate.reshape(local_heads * 3, fan_width, hid_width)
    for number in range(NS_ITERS):
        iterate = newton_step(iterate, iterate)
    iterate = iterate.reshape(local_heads, 3, fan_width, hid_width)
    updated = (
        fast_weights[0].astype(jnp.float32)
        - fast_rate[0][:, None, None, None] * iterate.astype(jnp.float32)
    ).astype(jnp.bfloat16)
    mixed_heads = apply_fast(queries, updated).reshape(tok_rows, half_width)
    partial_out = jnp.dot(
        mixed_heads,
        lax.all_gather(w_out[0], "tok", axis=1, tiled=True),
        preferred_element_type=jnp.float32,
    )
    summed_out = lax.psum_scatter(
        partial_out.astype(jnp.bfloat16), "head", scatter_dimension=1, tiled=True
    ).astype(jnp.float32)
    share_width = summed_out.shape[1]
    own_tokens = lax.dynamic_slice_in_dim(
        tokens, lax.axis_index("head") * share_width, share_width, 1
    )
    layer_out = (own_tokens.astype(jnp.float32) + summed_out).astype(jnp.bfloat16)
    handed = passed_along(layer_out[None], "section", 1)
    return (handed, updated[None])


def solution(mesh):
    placed = (
        P("section", "tok", None),
        P("section", None, "tok", "head"),
        P("section", "head", "tok"),
        P("section", "tok", "head"),
        P("section", "head", None, None, None),
        P("section", "head", None, None, None),
        P("section", "head"),
        P("section", "head"),
    )
    return jax.shard_map(
        shards,
        mesh=mesh,
        in_specs=placed,
        out_specs=(P("section", "tok", "head"), P("section", "head", None, None, None)),
        check_vma=False,
    )
```

profile of v0, /device:TPU:1, one launch (start us, length us, event | category | flops | bytes accessed | tf_op | source)
XLA Modules:
  0.0 474.2 jit_solution(7633743241635436623)
XLA Ops:
  7.2 0.0 all-gather.5.cloned.1.call-start
  7.2 4.6 copy.23
  11.8 0.0 copy-start.1
  11.8 0.0 all-gather.5.cloned.1.call-update
  11.9 0.0 all-reduce.2.cloned.1.call-start
  11.9 1.8 copy-done.1
  13.7 1.8 copy.51
  15.6 216.9 %all-gather.5.cloned.1.call-done = bf16[1,3,2048,1024]{2,3,1,0:T(8,128)(2,1)} async-done(((bf16[1,3,512,1024]{2,3,1,0:T(8,128)(2,1)}), bf16[1,3,2048,1024]{2,3,1,0:T(8,128)(2,1)}) %all-gather.5.cloned.1.call-update) | async-done | bytes 12582928 | tf_op jit(solution)/shard_map/all_gather | solution.py:85
  232.4 6.6 %fusion.19 = f32[3,128,1024]{1,2,0:T(8,128)S(1)} fusion(bf16[1,3,2048,1024]{2,3,1,0:T(8,128)(2,1)} %all-gather.5.cloned.1.call-done, bf16[1,128,2048]{2,1,0:T(8,128)(2,1)} %param.8), kind=kOutput, calls=%fused_computation.27 | convolution fusion | flops 1610612736 | bytes 14680064 | tf_op jit(solution)/shard_map/td,jde->jte/dot_general | solution.py:82
  239.0 0.0 copy-start.3
  239.0 0.9 fusion.47
  239.9 0.0 copy-start.9
  239.9 0.1 multiply_reduce_fusion.3
  240.1 1.0 copy-done.3
  241.1 0.3 convolution_bitcast_fusion.3
  241.5 0.3 convolution_bitcast_fusion.4
  241.8 0.0 copy-done.9
  241.9 0.3 convolution_bitcast_fusion.5
  242.2 0.5 fusion.23
  242.7 0.5 fusion.22
  243.2 0.5 fusion.24
  243.7 2.0 pad_maximum_fusion
  245.7 0.0 copy-start.4
  245.7 0.0 copy-start.8
  245.7 0.0 all-reduce.2.cloned.1.call-update
  245.7 0.0 all-gather.7.cloned.1.call-start
  245.8 0.7 all-gather.7.cloned.1.call-update
  246.5 0.2 reduce-scatter.2.cloned.1.call-start
  246.7 2.0 copy.31
  248.8 1.2 multiply_reduce_fusion.2
  249.9 114.9 %all-reduce.2.cloned.1.call-done = bf16[2,3,512,512]{3,2,0,1:T(8,128)(2,1)} async-done(((bf16[2,3,512,512]{3,2,0,1:T(8,128)(2,1)}), bf16[2,3,512,512]{3,2,0,1:T(8,128)(2,1)}) %all-reduce.2.cloned.1.call-update) | async-done | bytes 3145744 | tf_op jit(solution)/shard_map/psum | solution.py:94
  364.8 0.0 copy-done.4
  364.8 0.0 copy-done.8
  364.8 0.0 copy-start.5
  364.8 3.5 multiply_reduce_fusion
  368.3 0.0 copy-done.5
  368.3 1.3 divide_convert_fusion
  369.6 0.2 copy.27
  369.8 1.8 convolution_convert_fusion.1
  371.7 1.8 fusion.48
  373.5 2.2 add_convert_fusion.1
  375.7 1.8 convolution_convert_fusion
  377.5 1.8 fusion.49
  379.3 0.0 copy-start.7
  379.3 2.5 fusion.7
  381.9 0.0 copy-start
  381.9 0.0 copy-done.7
  381.9 0.0 copy-start.6
  381.9 5.4 %fusion.4 = bf16[2,3,512,512]{3,2,0,1:T(8,128)(2,1)S(1)} fusion(f32[2,3,512,512]{3,2,1,0:T(8,128)S(1)} %bitcast.108, f32[2]{0:T(128)S(1)} %bitcast.120, bf16[1,2,3,512,512]{4,3,2,1,0:T(8,128)(2,1)} %param.12), kind=kLoop, calls=%fused_computation.6 | loop fusion | flops 6291456 | bytes 12582920 | tf_op jit(solution)/shard_map/convert_element_type | solution.py:105
  387.3 0.0 copy-done
  387.3 0.0 copy-done.6
  387.3 1.1 convolution_bitcast_fusion.1
  388.4 2.8 multiply_reduce_fusion.1
  391.2 1.1 multiply_convert_fusion
  392.3 53.9 %all-gather.7.cloned.1.call-done = bf16[1,1024,2048]{2,1,0:T(8,128)(2,1)} async-done(((bf16[1,1024,512]{2,1,0:T(8,128)(2,1)}), bf16[1,1024,2048]{2,1,0:T(8,128)(2,1)}) %all-gather.7.cloned.1.call-update) | async-done | bytes 4194320 | tf_op jit(solution)/shard_map/all_gather | solution.py:109
  446.2 3.9 fusion.16
  450.1 0.0 reduce-scatter.2.cloned.1.call-update
  450.1 7.0 %reduce-scatter.2.cloned.1.call-done = bf16[128,1024]{1,0:T(8,128)(2,1)} async-done(((bf16[128,2048]{1,0:T(8,128)(2,1)}), bf16[128,1024]{1,0:T(8,128)(2,1)}) %reduce-scatter.2.cloned.1.call-update) | async-done | bytes 262160 | tf_op jit(solution)/shard_map/reduce_scatter | solution.py:112
  457.1 1.1 fusion.36
  458.2 1.6 collective-permute-start
  459.9 0.0 copy-done.2
  459.9 5.6 %subtract_convert_fusion = bf16[1,2,3,512,512]{4,3,2,1,0:T(8,128)(2,1)} fusion(f32[1,2,3,512,512]{4,3,2,1,0:T(8,128)} %bitcast.109, bf16[1,2,3,512,512]{4,3,2,1,0:T(8,128)(2,1)S(1)} %copy-done.2, f32[2]{0:T(128)S(1)} %bitcast.121), kind=kLoop, calls=%fused_computation.7 | loop fusion | flops 6291456 | bytes 12582920 | tf_op jit(solution)/shard_map/convert_element_type | solution.py:105
  465.4 1.6 collective-permute-done
  467.0 0.7 copy.54
  (7 shorter events, 0.1 us)
Async XLA Ops:
  7.2 225.3 %all-gather.5.cloned.1.call-start = ((), (), s32[]{:S(2)}) async-start(), calls=%async_computation.3 | async-start | bytes 15728640 | tf_op jit(solution)/shard_map/all_gather | solution.py:85
  11.8 1.9 copy-start.1
  11.9 352.9 %all-reduce.2.cloned.1.call-start = ((), (), s32[]{:S(2)}) async-start(), calls=%async_computation.1 | async-start | bytes 6291456 | tf_op jit(solution)/shard_map/psum | solution.py:94
  239.0 2.1 copy-start.3
  239.9 1.9 copy-start.9
  245.7 119.1 %copy-start.4 = (bf16[1,2,3,512,512]{4,3,2,1,0:T(8,128)(2,1)S(1)}, bf16[1,2,3,512,512]{4,3,2,1,0:T(8,128)(2,1)}, u32[]{:S(2)}) copy-start(bf16[1,2,3,512,512]{4,3,2,1,0:T(8,128)(2,1)} %param.13) | copy-start | bytes 9437188
  245.7 119.1 %copy-start.8 = (f32[1,2]{1,0:T(1,128)S(1)}, f32[1,2]{1,0:T(1,128)}, u32[]{:S(2)}) copy-start(f32[1,2]{1,0:T(1,128)} %param.14) | copy-start | bytes 28
  245.7 200.4 %all-gather.7.cloned.1.call-start = ((), (), s32[]{:S(2)}) async-start(), calls=%async_computation.4 | async-start | bytes 5242880 | tf_op jit(solution)/shard_map/all_gather | solution.py:109
  246.5 210.6 %reduce-scatter.2.cloned.1.call-start = ((), (), s32[]{:S(2)}) async-start(), calls=%async_computation.2 | async-start | bytes 786432 | tf_op jit(solution)/shard_map/reduce_scatter | solution.py:112
  364.8 3.5 copy-start.5
  379.3 2.5 copy-start.7
  381.9 5.4 %copy-start = (f32[6,512,512]{2,1,0:T(8,128)}, f32[6,512,512]{2,1,0:T(8,128)S(1)}, u32[]{:S(2)}) copy-start(f32[6,512,512]{2,1,0:T(8,128)S(1)} %fusion.7) | copy-start | bytes 18874372
  381.9 5.4 %copy-start.6 = (f32[128,2,512]{2,0,1:T(8,128)S(1)}, f32[128,2,512]{2,0,1:T(8,128)}, u32[]{:S(2)}) copy-start(f32[128,2,512]{2,0,1:T(8,128)} %copy.31) | copy-start | bytes 1572868
  446.2 13.7 %copy-start.2 = (bf16[1,2,3,512,512]{4,3,2,1,0:T(8,128)(2,1)S(1)}, bf16[1,2,3,512,512]{4,3,2,1,0:T(8,128)(2,1)}, u32[]{:S(2)}) copy-start(bf16[1,2,3,512,512]{4,3,2,1,0:T(8,128)(2,1)} %param.12) | copy-start | bytes 9437188
  458.2 8.7 %collective-permute-start = (bf16[1,128,1024]{2,1,0:T(8,128)(2,1)S(1)}, bf16[1,128,1024]{2,1,0:T(8,128)(2,1)S(1)}, u32[]{:S(2)}, u32[]{:S(2)}) collective-permute-start(bf16[1,128,1024]{2,1,0:T(8,128)(2,1)S(1)} %fusion.36), channel_id=1, source_target_pairs={{0,8},{8,16},{16,24},{24,0},{1,9},{9,17},{17,25},{25,1},{2,10},{10... | collective-permute-start | bytes 786440 | tf_op jit(solution)/shard_map/ppermute | solution.py:17
Sparse Core Ops, SparseCore 0:
  12.0 220.4 all-gather.4
  245.9 118.8 all-reduce.1
  366.4 79.7 all-gather.6
  450.2 6.8 reduce-scatter.1
where the time goes:
time: 476 us; the launch traced here: 474 us
  waiting for transfers between devices  395 us (83%)
  matrix products  28.9 us (6%)
  other arithmetic  21.2 us (4%)
  between operations  14 us (3%)
  local copies, waits for them, and re-layouts  13.2 us (3%)
    all_gather x1, waiting for transfers between devices, shards(): lax.all_gather(w_qkv[0], 'tok', axis=1, tiled=True)  217 us
    psum x1, waiting for transfers between devices, shards(): summed = lax.psum(gradients.astype(jnp.bfloat16), 'tok').astype(jnp.float32)  115 us
    all_gather x1, waiting for transfers between devices, shards(): lax.all_gather(w_out[0], 'tok', axis=1, tiled=True)  53.9 us
    convert_element_type x2, other arithmetic, shards(): updated = (fast_weights[0].astype(jnp.float32) - fast_rate[0][:, None, No...  10.9 us
    unnamed x23, local copies, waits for them, and re-layouts  10.1 us
  transfers between devices with their start and end apart: 5, of which 5 were waited for; matrix products, arithmetic and copies ran while one was open for 8% of the time, Pallas kernels for 0%

commit v1 on v0

--- a/solution.py
+++ b/solution.py
@@ -79,19 +79,25 @@
     fan_width = fast_weights.shape[3]
     hid_width = fast_weights.shape[4]
     half_width = w_qkv.shape[3]
-    projected = jnp.einsum(
-        "td,jde->jte",
-        tokens,
-        lax.all_gather(w_qkv[0], "tok", axis=1, tiled=True),
-        preferred_element_type=jnp.float32,
+    columns = lax.all_to_all(tokens, "tok", split_axis=1, concat_axis=0, tiled=True)
+    all_rows = columns.shape[0]
+    rates = lax.all_gather(step_sizes[0], "tok", axis=0, tiled=True)
+    partial_kv = jnp.einsum(
+        "td,jde->jte", columns, w_qkv[0, 1:], preferred_element_type=jnp.float32
+    ).astype(jnp.bfloat16)
+    partial_q = jnp.dot(columns, w_qkv[0, 0], preferred_element_type=jnp.float32).astype(
+        jnp.bfloat16
     )
-    shaped = projected.reshape(3, tok_rows, local_heads, fan_width)
-    queries = rms_rows(shaped[0], 1e-06).astype(jnp.bfloat16)
-    key_rows = rms_rows(shaped[1], 1e-06).astype(jnp.bfloat16)
-    value_rows = shaped[2].astype(jnp.bfloat16)
-    gradients = fast_grads(key_rows, value_rows, step_sizes[0], fast_weights[0])
+    summed_kv = lax.psum(partial_kv, "tok").astype(jnp.float32)
+    summed_q = lax.psum(partial_q, "tok").astype(jnp.float32)
+    shaped = summed_kv.reshape(2, all_rows, local_heads, fan_width)
+    key_rows = rms_rows(shaped[0], 1e-06).astype(jnp.bfloat16)
+    value_rows = shaped[1].astype(jnp.bfloat16)
+    queries = rms_rows(summed_q.reshape(all_rows, local_heads, fan_width), 1e-06).astype(
+        jnp.bfloat16
+    )
+    summed = fast_grads(key_rows, value_rows, rates, fast_weights[0])
     decay_rate = momentum_decay[0][:, None, None, None]
-    summed = lax.psum(gradients.astype(jnp.bfloat16), "tok").astype(jnp.float32)
     moment = decay_rate * momentum[0].astype(jnp.float32) + summed
     norm_values = jnp.sqrt(jnp.sum(moment * moment, axis=(2, 3), keepdims=True))
     iterate = (moment / (norm_values + 1e-06)).astype(jnp.bfloat16)
@@ -103,15 +109,14 @@
         fast_weights[0].astype(jnp.float32)
         - fast_rate[0][:, None, None, None] * iterate.astype(jnp.float32)
     ).astype(jnp.bfloat16)
-    mixed_heads = apply_fast(queries, updated).reshape(tok_rows, half_width)
-    partial_out = jnp.dot(
-        mixed_heads,
-        lax.all_gather(w_out[0], "tok", axis=1, tiled=True),
-        preferred_element_type=jnp.float32,
+    mixed_heads = apply_fast(queries, updated).reshape(all_rows, half_width)
+    partial_out = jnp.dot(mixed_heads, w_out[0], preferred_element_type=jnp.float32)
+    own_rows = lax.all_to_all(
+        partial_out.astype(jnp.bfloat16), "tok", split_axis=0, concat_axis=1, tiled=True
     )
-    summed_out = lax.psum_scatter(
-        partial_out.astype(jnp.bfloat16), "head", scatter_dimension=1, tiled=True
-    ).astype(jnp.float32)
+    summed_out = lax.psum_scatter(own_rows, "head", scatter_dimension=1, tiled=True).astype(
+        jnp.float32
+    )
     share_width = summed_out.shape[1]
     own_tokens = lax.dynamic_slice_in_dim(
         tokens, lax.axis_index("head") * share_width, share_width, 1

time: 476 us -> 257 us (0.54)
  waiting for transfers between devices: 395 us -> 112 us
  blocking collectives: 0 us -> 43.3 us
  matrix products: 28.9 us -> 37.3 us
  local copies, waits for them, and re-layouts: 13.2 us -> 20 us
  other arithmetic: 21.2 us -> 26.1 us
    all_gather x2 -> x0, waiting for transfers between devices: 271 us -> none  [the longest x1 217 us: shards(): lax.all_gather(w_qkv[0], 'tok', axis=1, tiled=True)]
    all_to_all x0 -> x2, blocking collectives: none -> 35.3 us  [the longest x1 19.2 us: shards(): lax.all_to_all(tokens, 'tok', split_axis=1, concat_axis=0, tiled=True)]
    psum x1, waiting for transfers between devices: 115 us -> 103 us  [shards(): summed_kv = lax.psum(partial_kv, 'tok').astype(jnp.float32)]
    all_gather x0 -> x1, blocking collectives: none -> 8.08 us  [shards(): rates = lax.all_gather(step_sizes[0], 'tok', axis=0, tiled=True)]
    dot_general x2 -> x3, matrix products: 10.5 us -> 5.37 us  [the longest x1 2.69 us: shards(): jnp.einsum('td,jde->jte', columns, w_qkv[0, 1:], preferred_element_type=j...]
    convert_element_type x1, other arithmetic: 1.29 us -> 6.36 us  [shards(): iterate = (moment / (norm_values + 1e-06)).astype(jnp.bfloat16)]
    unnamed x23 -> x24, local copies, waits for them, and re-layouts: 10.1 us -> 7.67 us
  transfers between devices with their start and end apart: 5 -> 3, of which waited for: 5 -> 3; matrix products, arithmetic and copies ran while one was open for 8% -> 7% of each run, Pallas kernels for 0% -> 0%
where the time goes in v1:
time: 257 us; the launch traced here: 255 us
  waiting for transfers between devices  112 us (44%)
  blocking collectives  43.3 us (17%)
  matrix products  37.3 us (15%)
  other arithmetic  26.1 us (10%)
  local copies, waits for them, and re-layouts  20 us (8%)
  between operations  14.3 us (6%)
    psum x1, waiting for transfers between devices, shards(): summed_kv = lax.psum(partial_kv, 'tok').astype(jnp.float32)  103 us
    all_to_all x1, blocking collectives, shards(): lax.all_to_all(tokens, 'tok', split_axis=1, concat_axis=0, tiled=True)  19.2 us
    all_to_all x1, blocking collectives, shards(): lax.all_to_all(partial_out.astype(jnp.bfloat16), 'tok', split_axis=0, con...  16.1 us
    convert_element_type x2, other arithmetic, shards(): updated = (fast_weights[0].astype(jnp.float32) - fast_rate[0][:, None, No...  11.5 us
    dot_general x2, matrix products, newton_step(): jnp.einsum('mij,mjk->mik', cubic_term.astype(jnp.bfloat16), gram_matrix,...  9.3 us
    reduce_scatter x1, waiting for transfers between devices, shards(): lax.psum_scatter(own_rows, 'head', scatter_dimension=1, tiled=True)  8.58 us
    all_gather x1, blocking collectives, shards(): rates = lax.all_gather(step_sizes[0], 'tok', axis=0, tiled=True)  8.08 us
    unnamed x24, local copies, waits for them, and re-layouts  7.67 us
  transfers between devices with their start and end apart: 3, of which 3 were waited for; matrix products, arithmetic and copies ran while one was open for 7% of the time, Pallas kernels for 0%

profile of v1, /device:TPU:1, one launch (start us, length us, event | category | flops | bytes accessed | tf_op | source)
XLA Modules:
  0.0 255.0 jit_solution(371909318707594207)
XLA Ops:
  7.2 0.0 copy-start
  7.2 0.0 all-reduce.3.cloned.1.call-start
  7.2 1.5 all_to_all.28
  8.7 0.1 copy.43
  8.8 0.0 copy-start.10
  8.9 19.2 %all_to_all.38 = bf16[128,4,512]{2,0,1:T(8,128)(2,1)S(1)} all-to-all(bf16[128,4,512]{2,0,1:T(8,128)(2,1)S(1)} %copy.43), channel_id=1, replica_groups=mesh['section'=4,'tok'=4,'head'=2] {'tok'}, dimensions={1} | all-to-all | bytes 1048576 | tf_op jit(solution)/shard_map/all_to_all | solution.py:82
  28.0 1.9 convolution_convert_fusion.2
  30.0 1.1 copy.83
  31.0 0.0 copy-done.10
  31.0 2.7 %convert_bitcast_fusion = bf16[2,512,1024]{1,2,0:T(8,128)(2,1)} fusion(bf16[512,512,1]{1,0,2:T(8,128)(2,1)S(1)} %bitcast.205, bf16[1,3,512,1024]{3,2,1,0:T(8,128)(2,1)S(1)} %copy-done.10), kind=kOutput, calls=%fused_computation.64 | convolution fusion | flops 1074790400 | bytes 4718592 | tf_op jit(solution)/shard_map/td,jde->jte/dot_general | solution.py:85
  33.7 0.0 all-reduce.3.cloned.1.call-update
  33.7 0.0 copy-start.9
  33.7 0.0 reduce-scatter.2.cloned.1.call-start
  33.8 3.9 %copy.82 = bf16[1,2,3,512,512]{4,3,1,2,0:T(8,128)(2,1)} copy(bf16[1,2,3,512,512]{4,3,2,1,0:T(8,128)(2,1)} %param.12) | data formatting | bytes 6291456 | tf_op args[4]
  37.7 0.0 copy-done.9
  37.7 0.1 mul.144
  37.8 0.1 mul.145
  37.9 2.8 %copy_convert_fusion = f32[1,2,3,512,512]{4,3,1,2,0:T(8,128)S(1)} fusion(bf16[1,2,3,512,512]{4,3,2,1,0:T(8,128)(2,1)} %param.13), kind=kLoop, calls=%fused_computation.16 | loop fusion | flops 1572864 | bytes 9437184 | tf_op jit(solution)/shard_map/convert_element_type | solution.py:101
  40.7 0.0 copy-start.8
  40.7 3.4 %copy.41 = f32[1,2,3,512,512]{4,3,2,1,0:T(8,128)} copy(f32[1,2,3,512,512]{4,3,1,2,0:T(8,128)S(1)} %copy_convert_fusion) | data formatting | bytes 12582912 | tf_op jit(solution)/shard_map/convert_element_type | solution.py:101
  44.0 8.1 %all-gather = f32[1,512,2]{1,2,0:T(2,128)S(1)} all-gather(f32[1,128,2]{1,2,0:T(2,128)S(1)} %copy-done.8), channel_id=2, replica_groups=mesh['section'=4,'tok'=4,'head'=2] {'tok'}, dimensions={1}, use_global_device_ids=true | all-gather | bytes 5120 | tf_op jit(solution)/shard_map/all_gather | solution.py:84
  52.1 102.9 %all-reduce.3.cloned.1.call-done = (bf16[2,512,1024]{1,2,0:T(8,128)(2,1)}, bf16[512,2,512]{2,0,1:T(8,128)(2,1)}) async-done(((bf16[2,512,1024]{1,2,0:T(8,128)(2,1)}, bf16[512,2,512]{2,0,1:T(8,128)(2,1)}), (bf16[2,512,1024]{1,2,0:T(8,128)(2,1)}, bf16[512,2,512]{2,0,1:T(8,128)(2,1)})) %all-reduce.3.cloned.1.call-update) | async-done | bytes 3145744 | tf_op jit(solution)/shard_map/psum | solution.py:91
  155.0 1.8 fusion.71
  156.8 0.2 fusion.18
  157.1 0.4 copy-done.3
  157.5 0.8 fusion.46
  158.3 0.8 fusion.47
  159.0 0.8 fusion.48
  159.8 1.0 convolution_bitcast_fusion.1
  160.8 1.3 convolution_bitcast_fusion.2
  162.1 0.0 copy-start.2
  162.1 1.0 convolution_bitcast_fusion
  163.1 0.9 copy-done.2
  164.0 2.1 fusion.2
  166.1 3.4 %copy.47 = f32[2,3,512,512]{3,2,1,0:T(8,128)} copy(f32[2,3,512,512]{3,2,0,1:T(8,128)S(1)} %get-tuple-element.5) | data formatting | bytes 12582912 | tf_op jit(solution)/shard_map/stack | solution.py:42
  169.4 0.1 copy.48
  169.5 0.1 add.85
  169.6 6.4 %fusion.4 = bf16[6,512,512]{2,1,0:T(8,128)(2,1)S(1)} fusion(f32[2,3,512,512]{3,2,1,0:T(8,128)} %copy.47, f32[1,2,3,512,512]{4,3,2,1,0:T(8,128)} %copy.41, f32[6]{0:T(128)S(1)} %add.85, f32[6]{0:T(128)S(1)} %mul.145), kind=kLoop, calls=%fused_computation.7 | loop fusion | flops 6291456 | bytes 15728688 | tf_op jit(solution)/shard_map/convert_element_type | solution.py:103
  176.0 1.8 convolution_convert_fusion.1
  177.8 4.5 %fusion.74 = f32[6,512,512]{2,1,0:T(8,128)} fusion(bf16[6,512,512]{2,1,0:T(8,128)(2,1)S(1)} %fusion.4, bf16[6,512,512]{2,1,0:T(8,128)(2,1)S(1)} %convolution_convert_fusion.1), kind=kOutput, calls=%fused_computation.99 | convolution fusion | flops 1610612736 | bytes 12582912 | tf_op jit(solution)/shard_map/mij,mjk->mik/dot_general | solution.py:49
  182.3 6.9 %add_convert_fusion.1 = bf16[6,512,512]{2,1,0:T(8,128)(2,1)S(1)} fusion(f32[6,512,512]{2,1,0:T(8,128)} %fusion.74, bf16[6,512,512]{2,1,0:T(8,128)(2,1)S(1)} %fusion.4, bf16[6,512,512]{2,1,0:T(8,128)(2,1)S(1)} %convolution_convert_fusion.1), kind=kOutput, calls=%fused_computation.14 | convolution fusion | flops 1623195648 | bytes 15728640 | tf_op jit(solution)/shard_map/mij,mjk->mik/dot_general | solution.py:52
  189.1 1.8 convolution_convert_fusion
  191.0 1.8 fusion.75
  192.8 0.0 copy-start.7
  192.8 2.4 fusion.7
  195.3 0.3 fusion.16
  195.6 0.0 copy-done.7
  195.6 5.0 %fusion.6 = bf16[2,3,512,512]{3,2,0,1:T(8,128)(2,1)S(1)} fusion(f32[2,3,512,512]{3,2,1,0:T(8,128)S(1)} %bitcast.187, f32[2]{0:T(128)S(1)} %bitcast.209, bf16[1,2,3,512,512]{4,3,2,1,0:T(8,128)(2,1)} %param.12), kind=kLoop, calls=%fused_computation.11 | loop fusion | flops 6291456 | bytes 12582920 | tf_op jit(solution)/shard_map/convert_element_type | solution.py:111
  200.6 0.0 copy-start.4
  200.6 1.7 copy-done.4
  202.3 2.1 fusion.45
  204.4 5.1 %fusion.24 = (f32[512,2]{0,1:T(2,128)S(1)}, f32[2,512,512]{2,1,0:T(8,128)}) fusion(f32[2,512,512]{1,2,0:T(8,128)} %fusion.45, bf16[2,3,512,512]{3,2,0,1:T(8,128)(2,1)} %copy-done.4, bf16[512,2,512]{2,0,1:T(8,128)(2,1)S(1)} %copy-done.5, f32[512,2]{0,1:T(2,128)S(1)} %add_rsqrt_fusion.1), kind=kOutput, calls=%fused_computation.39 | convolution fusion | flops 1079507968 | bytes 7348224 | tf_op jit(solution)/shard_map/thj,hij->thi/dot_general | solution.py:71
  209.5 1.9 fusion.25
  211.4 0.0 copy-start.6
  211.4 0.7 convolution_convert_fusion.3
  212.2 16.1 %all_to_all.39 = bf16[4,128,512]{2,1,0:T(8,128)(2,1)S(1)} all-to-all(bf16[4,128,512]{2,1,0:T(8,128)(2,1)S(1)} %bitcast.206), channel_id=1, replica_groups=mesh['section'=4,'tok'=4,'head'=2] {'tok'}, dimensions={0} | all-to-all | bytes 1048576 | tf_op jit(solution)/shard_map/all_to_all | solution.py:114
  228.3 0.8 copy.69
  229.1 0.0 reduce-scatter.2.cloned.1.call-update
  229.1 8.6 %reduce-scatter.2.cloned.1.call-done = bf16[128,1024]{1,0:T(8,128)(2,1)} async-done(((bf16[128,2048]{1,0:T(8,128)(2,1)}), bf16[128,1024]{1,0:T(8,128)(2,1)}) %reduce-scatter.2.cloned.1.call-update) | async-done | bytes 262160 | tf_op jit(solution)/shard_map/reduce_scatter | solution.py:117
  237.7 1.0 fusion.66
  238.7 1.6 collective-permute-start
  240.3 6.5 %subtract_convert_fusion = bf16[1,2,3,512,512]{4,3,2,1,0:T(8,128)(2,1)} fusion(f32[1,2,3,512,512]{4,3,2,1,0:T(8,128)} %bitcast.188, bf16[1,2,3,512,512]{4,3,2,1,0:T(8,128)(2,1)} %param.12, f32[2]{0:T(128)S(1)} %bitcast.210), kind=kLoop, calls=%fused_computation.12 | loop fusion | flops 6291456 | bytes 12582920 | tf_op jit(solution)/shard_map/convert_element_type | solution.py:111
  246.8 0.6 collective-permute-done
  247.5 0.7 copy.87
  (12 shorter events, 0.1 us)
Async XLA Ops:
  7.2 204.2 %copy-start = (bf16[1,1024,512]{2,1,0:T(8,128)(2,1)S(1)}, bf16[1,1024,512]{2,1,0:T(8,128)(2,1)}, u32[]{:S(2)}) copy-start(bf16[1,1024,512]{2,1,0:T(8,128)(2,1)} %param.10) | copy-start | bytes 3145732
  7.2 147.8 %all-reduce.3.cloned.1.call-start = ((), (), s32[]{:S(2)}) async-start(), calls=%async_computation.4 | async-start | bytes 6291456 | tf_op jit(solution)/shard_map/psum | solution.py:91
  8.8 22.2 %copy-start.10 = (bf16[1,3,512,1024]{3,2,1,0:T(8,128)(2,1)S(1)}, bf16[1,3,512,1024]{3,2,1,0:T(8,128)(2,1)}, u32[]{:S(2)}) copy-start(bf16[1,3,512,1024]{3,2,1,0:T(8,128)(2,1)} %param.9) | copy-start | bytes 9437188
  33.7 4.0 %copy-start.9 = (f32[1,2]{1,0:T(1,128)S(1)}, f32[1,2]{1,0:T(1,128)}, u32[]{:S(2)}) copy-start(f32[1,2]{1,0:T(1,128)} %param.14) | copy-start | bytes 28
  33.7 204.0 %reduce-scatter.2.cloned.1.call-start = ((), (), s32[]{:S(2)}) async-start(), calls=%async_computation.3 | async-start | bytes 786432 | tf_op jit(solution)/shard_map/reduce_scatter | solution.py:117
  40.7 3.4 %copy-start.8 = (f32[1,128,2]{1,2,0:T(2,128)S(1)}, f32[1,128,2]{1,2,0:T(2,128)}, u32[]{:S(2)}) copy-start(f32[1,128,2]{1,2,0:T(2,128)} %param.11) | copy-start | bytes 3076
  155.0 2.5 copy-start.3
  162.1 1.9 copy-start.2
  192.8 2.5 copy-start.5
  192.8 2.8 %copy-start.7 = (f32[1,2]{1,0:T(1,128)S(1)}, f32[1,2]{1,0:T(1,128)}, u32[]{:S(2)}) copy-start(f32[1,2]{1,0:T(1,128)} %param.15) | copy-start | bytes 28
  195.2 5.4 %copy-start.1 = (f32[6,512,512]{2,1,0:T(8,128)}, f32[6,512,512]{2,1,0:T(8,128)S(1)}, u32[]{:S(2)}) copy-start(f32[6,512,512]{2,1,0:T(8,128)S(1)} %fusion.7) | copy-start | bytes 18874372
  200.6 1.7 copy-start.4
  211.4 26.3 %copy-start.6 = (bf16[1,128,2048]{2,1,0:T(8,128)(2,1)S(1)}, bf16[1,128,2048]{2,1,0:T(8,128)(2,1)}, u32[]{:S(2)}) copy-start(bf16[1,128,2048]{2,1,0:T(8,128)(2,1)} %param.8) | copy-start | bytes 1572868
  238.7 8.7 %collective-permute-start = (bf16[1,128,1024]{2,1,0:T(8,128)(2,1)S(1)}, bf16[1,128,1024]{2,1,0:T(8,128)(2,1)S(1)}, u32[]{:S(2)}, u32[]{:S(2)}) collective-permute-start(bf16[1,128,1024]{2,1,0:T(8,128)(2,1)S(1)} %fusion.66), channel_id=1, source_target_pairs={{0,8},{8,16},{16,24},{24,0},{1,9},{9,17},{17,25},{25,1},{2,10},{10... | collective-permute-start | bytes 786440 | tf_op jit(solution)/shard_map/ppermute | solution.py:17
Sparse Core Ops, SparseCore 0:
  33.9 121.0 all-reduce.2
  229.2 8.4 reduce-scatter.1

commit v2 on v1

--- a/solution.py
+++ b/solution.py
@@ -1,6 +1,10 @@
+import functools
+
 import jax
 import jax.numpy as jnp
 from jax import lax
+from jax.experimental import pallas as pl
+from jax.experimental.pallas import tpu as pltpu
 from jax.sharding import PartitionSpec as P
 
 NS_ITERS = 2
@@ -72,7 +76,7 @@
     return rms_rows(output, 1e-05).astype(jnp.bfloat16)
 
 
-def shards(group_in, w_qkv, w_out, step_sizes, fast_weights, momentum, momentum_decay, fast_rate):
+def plain_shards(group_in, w_qkv, w_out, step_sizes, fast_weights, momentum, momentum_decay, fast_rate):
     tokens = group_in[0]
     tok_rows = tokens.shape[0]
     local_heads = fast_weights.shape[1]
@@ -126,6 +130,421 @@
     return (handed, updated[None])
 
 
+MESH = pl.DeviceIdType.MESH
+F32 = jnp.float32
+BF16 = jnp.bfloat16
+CHUNK = 32
+QUERY_CHUNK = 64
+
+
+def dot(a, b, a_dim=1, b_dim=0):
+    return lax.dot_general(a, b, (((a_dim,), (b_dim,)), ((), ())), preferred_element_type=F32)
+
+
+def layer_kernel(
+    dims, x_ref, rate_ref, decay_ref, fast_rate_ref, wqkv_hbm, wout_hbm, fast_hbm, mom_hbm,
+    handed_ref, next_hbm,
+    wqkv, wout, fast, mom, moved, columns, rates, rate_in, part, outer_in, cross_in, final,
+    qpart, qouter_in, qcross_in, qfinal, grad, updated, mixed, half_out, half_in, sent, hand,
+    load_sem, x_send, x_recv, fwd_send, fwd_recv, rate_send, rate_recv,
+    s_send, o_recv, c_recv, f_send, f_recv, qs_send, qo_recv, qc_recv, qf_send, qf_recv,
+    next_sem, half_send, half_recv, hand_send, hand_recv,
+):
+    sections, n, heads, fin, hid = dims
+    rows = x_ref.shape[0]
+    width = columns.shape[3]
+    half = rows // 2
+    all_rows = rows * n
+    local = heads * fin
+    per_block = rows // CHUNK
+    chunks = n * per_block
+    qchunks = all_rows // QUERY_CHUNK
+    sec, me, core = lax.axis_index("section"), lax.axis_index("tok"), lax.axis_index("head")
+    mate = 1 - core
+    right = me // (n // 2)
+    inner, outer = me + 1 - 2 * right, me - 1 + 2 * right
+    is_end = (me == 0) | (me == n - 1)
+    is_mid = (me == n // 2 - 1) | (me == n // 2)
+    share = n // 2
+    next_sec, last_sec = lax.rem(sec + 1, sections), lax.rem(sec + sections - 1, sections)
+    peers = [lax.rem(me + step, n) for step in range(1, n)]
+
+    loads = [
+        pltpu.make_async_copy(src, dst, load_sem.at[i])
+        for i, (src, dst) in enumerate(
+            [(wqkv_hbm, wqkv), (fast_hbm, fast), (mom_hbm, mom), (wout_hbm, wout)]
+        )
+    ]
+    for load in loads:
+        load.start()
+
+    barrier = pltpu.get_barrier_semaphore()
+
+    def greet(device):
+        pl.semaphore_signal(barrier, inc=1, device_id=device, device_id_type=MESH)
+
+    for peer in peers:
+        greet((sec, peer, core))
+    greet((sec, me, mate))
+    for j in range(share):
+        greet((next_sec, core * share + j, me // share))
+        greet((last_sec, core * share + j, me // share))
+    pl.semaphore_wait(barrier, n + 2 * share)
+
+    def remote(src, dst, send, recv, device):
+        return pltpu.make_async_remote_copy(
+            src_ref=src, dst_ref=dst, send_sem=send, recv_sem=recv,
+            device_id=device, device_id_type=MESH,
+        )
+
+    def x_copy(peer):
+        start = pl.multiple_of(peer * width, 128)
+        return remote(
+            x_ref.at[pl.ds(core * half, half), pl.ds(start, width)], columns.at[me, core],
+            x_send.at[peer], x_recv.at[me], (sec, peer, core),
+        )
+
+    def x_from(source):
+        return remote(
+            columns.at[source, core], columns.at[source, core],
+            x_send.at[source], x_recv.at[source], (sec, source, core),
+        )
+
+    def x_forward(source):
+        return remote(
+            columns.at[source, core], columns.at[source, core],
+            fwd_send.at[source], fwd_recv.at[source], (sec, me, mate),
+        )
+
+    def x_forwarded(source):
+        return remote(
+            columns.at[source, mate], columns.at[source, mate],
+            fwd_send.at[source], fwd_recv.at[source], (sec, me, mate),
+        )
+
+    def rate_copy(peer, slot):
+        return remote(
+            rate_ref, rate_in.at[slot], rate_send.at[peer], rate_recv.at[slot], (sec, peer, core)
+        )
+
+    for peer in peers:
+        x_copy(peer).start()
+        rate_copy(peer, me).start()
+    own = x_ref[:, pl.ds(pl.multiple_of(me * width, 128), width)]
+    columns[me] = own.reshape(2, half, width)
+
+    def normed(values, epsilon):
+        return values * lax.rsqrt(jnp.mean(values * values, axis=-1, keepdims=True) + epsilon)
+
+    def stages(part, outer_in, cross_in, final, s_send, o_recv, c_recv, f_send, f_recv, finish):
+        def to_outer_in(c):
+            return remote(part.at[c], outer_in.at[c], s_send.at[c], o_recv.at[c], (sec, inner, core))
+
+        def to_cross_in(c):
+            return remote(part.at[c], cross_in.at[c], s_send.at[c], c_recv.at[c], (sec, inner, core))
+
+        def outward(c):
+            return remote(final.at[c], final.at[c], f_send.at[c], f_recv.at[c], (sec, outer, core))
+
+        def gather(c):
+            @pl.when(jnp.logical_not(is_end))
+            def _():
+                to_outer_in(c).wait_recv()
+                part[c] = (part[c].astype(F32) + outer_in[c].astype(F32)).astype(BF16)
+
+            @pl.when(is_mid)
+            def _():
+                to_cross_in(c).start()
+
+            @pl.when(jnp.logical_not(is_mid))
+            def _():
+                to_outer_in(c).start()
+
+        def spread(c):
+            @pl.when(is_mid)
+            def _():
+                to_cross_in(c).wait_recv()
+                finish(c, part[c].astype(F32) + cross_in[c].astype(F32))
+
+            @pl.when(jnp.logical_not(is_mid))
+            def _():
+                outward(c).wait_recv()
+
+            @pl.when(jnp.logical_not(is_end))
+            def _():
+                outward(c).start()
+
+        def drain(c):
+            to_outer_in(c).wait_send()
+
+            @pl.when(jnp.logical_not(is_end))
+            def _():
+                outward(c).wait_send()
+
+        return gather, spread, drain
+
+    def finish_kv(c, total):
+        block, row = c // per_block, (c % per_block) * CHUNK
+        for h in range(heads):
+            lanes = slice(h * fin, (h + 1) * fin)
+            final[c, :, lanes] = normed(total[:, lanes], 1e-06).astype(BF16)
+            value = total[:, local + h * fin : local + (h + 1) * fin].astype(BF16).astype(F32)
+            rate = rates[h, block, pl.ds(pl.multiple_of(row, CHUNK), CHUNK), :][:, :1]
+            final[c, :, local + h * fin : local + (h + 1) * fin] = (-(rate * value)).astype(BF16)
+
+    def finish_q(c, total):
+        for h in range(heads):
+            lanes = slice(h * fin, (h + 1) * fin)
+            qfinal[c, :, lanes] = normed(total[:, lanes], 1e-06).astype(BF16)
+
+    gather, spread, drain = stages(
+        part, outer_in, cross_in, final, s_send, o_recv, c_recv, f_send, f_recv, finish_kv
+    )
+    qgather, qspread, qdrain = stages(
+        qpart, qouter_in, qcross_in, qfinal, qs_send, qo_recv, qc_recv, qf_send, qf_recv, finish_q
+    )
+
+    for block in range(n):
+        @pl.when(me != block)
+        def _():
+            x_from(block).wait_recv()
+            x_forward(block).start()
+            rate_copy(block, block).wait_recv()
+            x_forwarded(block).wait_recv()
+            for h in range(heads):
+                line = rate_in[block, h : h + 1, :]
+                rates[h, block] = jnp.transpose(jnp.broadcast_to(line, (rows, rows)))
+
+        @pl.when(me == block)
+        def _():
+            for h in range(heads):
+                line = rate_ref[h : h + 1, :]
+                rates[h, block] = jnp.transpose(jnp.broadcast_to(line, (rows, rows)))
+
+        if block == 0:
+            loads[0].wait()
+        tile = columns[block].reshape(rows, width)
+        for j in range(2):
+            made = dot(tile, wqkv[j + 1]).astype(BF16).reshape(per_block, CHUNK, local)
+            part[block * per_block : (block + 1) * per_block, :, j * local : (j + 1) * local] = made
+
+        @pl.loop(block * per_block, (block + 1) * per_block)
+        def _(c):
+            gather(c)
+
+            @pl.when(c >= 2)
+            def _():
+                spread(c - 2)
+
+    tile = columns[...].reshape(all_rows, width)
+    qpart[...] = dot(tile, wqkv[0]).astype(BF16).reshape(qchunks, QUERY_CHUNK, local)
+
+    @pl.when(is_end)
+    def _():
+        @pl.loop(0, qchunks)
+        def _(c):
+            qgather(c)
+
+    spread(chunks - 2)
+    spread(chunks - 1)
+
+    def query_step(c):
+        @pl.when(jnp.logical_not(is_end) & (c < qchunks))
+        def _():
+            qgather(c)
+
+        @pl.when(jnp.logical_not(is_end) & (c >= 2) & (c < qchunks + 2))
+        def _():
+            qspread(c - 2)
+
+    loads[1].wait()
+    loads[2].wait()
+
+    def store_next(m):
+        return pltpu.make_async_copy(updated.at[m], next_hbm.at[m], next_sem.at[m])
+
+    @pl.loop(0, heads)
+    def _(h):
+        lanes = pl.ds(pl.multiple_of(h * fin, 128), fin)
+        err_lanes = pl.ds(pl.multiple_of(local + h * fin, 128), fin)
+        keys = final[:, :, lanes].reshape(all_rows, fin)
+        errors = final[:, :, err_lanes].reshape(all_rows, fin)
+        gate = dot(keys, fast[h * 3])
+        squash = jax.nn.sigmoid(gate)
+        up = dot(keys, fast[h * 3 + 1])
+        hidden = (gate * squash * up).astype(BF16)
+        back = dot(errors, fast[h * 3 + 2])
+        grad_gate = (back * up * squash * (1.0 + gate * (1.0 - squash))).astype(BF16)
+        grad_up = (back * gate * squash).astype(BF16)
+        grad[0] = dot(keys, grad_gate, 0, 0)
+        grad[1] = dot(keys, grad_up, 0, 0)
+        grad[2] = dot(errors, hidden, 0, 0)
+
+        @pl.loop(0, 3)
+        def _(j):
+            m = h * 3 + j
+            moment = decay_ref[h] * mom[m].astype(F32) + grad[j]
+            size = jnp.sqrt(jnp.sum(moment * moment))
+            moved[...] = (moment / (size + 1e-06)).astype(BF16)
+            for _ in range(NS_ITERS):
+                it = moved[...]
+                gram = dot(it, it, 0, 0).astype(BF16)
+                cubic = dot(it, gram)
+                quintic = dot(cubic.astype(BF16), gram)
+                moved[...] = (
+                    coef_linear * it.astype(F32) + coef_cubic * cubic + coef_quintic * quintic
+                ).astype(BF16)
+            updated[m] = (
+                fast[m].astype(F32) - fast_rate_ref[h] * moved[...].astype(F32)
+            ).astype(BF16)
+            store_next(m).start()
+            query_step(m)
+
+    @pl.loop(heads * 3, qchunks + 2)
+    def _(c):
+        query_step(c)
+
+    @pl.when(is_end)
+    def _():
+        @pl.loop(0, qchunks)
+        def _(c):
+            qspread(c)
+
+    @pl.loop(0, heads)
+    def _(h):
+        lanes = pl.ds(pl.multiple_of(h * fin, 128), fin)
+        queries = qfinal[:, :, lanes].reshape(all_rows, fin)
+        gate = dot(queries, updated[h * 3])
+        up = dot(queries, updated[h * 3 + 1])
+        hidden = (gate * jax.nn.sigmoid(gate) * up).astype(BF16)
+        output = dot(hidden, updated[h * 3 + 2], 1, 1)
+        mixed[:, lanes] = normed(output, 1e-05).astype(BF16)
+
+    loads[3].wait()
+    span = all_rows // 2
+    mine = pl.ds(pl.multiple_of(core * span, 128), span)
+    theirs = pl.ds(pl.multiple_of(mate * span, 128), span)
+    half_out[...] = dot(mixed[theirs, :], wout[...]).astype(BF16)
+    swap = remote(half_out, half_in, half_send, half_recv, (sec, me, mate))
+    swap.start()
+    summed = dot(mixed[mine, :], wout[...])
+    residual = columns[pl.ds(core * share, share)].reshape(span, width).astype(F32)
+    swap.wait()
+    sent[...] = (residual + (summed + half_in[...].astype(F32))).astype(BF16).reshape(
+        share, rows, width
+    )
+
+    def hand_over(j, slot):
+        return remote(
+            sent.at[j], hand.at[slot], hand_send.at[j], hand_recv.at[slot],
+            (next_sec, core * share + j, me // share),
+        )
+
+    for j in range(share):
+        hand_over(j, lax.rem(me, share)).start()
+    for peer in peers:
+        x_copy(peer).wait_send()
+        rate_copy(peer, me).wait_send()
+        x_forward(peer).wait_send()
+
+    @pl.loop(0, chunks)
+    def _(c):
+        drain(c)
+
+    @pl.loop(0, qchunks)
+    def _(c):
+        qdrain(c)
+
+    for m in range(heads * 3):
+        store_next(m).wait()
+    for j in range(share):
+        hand_over(j, j).wait_recv()
+        handed_ref[:, j * width : (j + 1) * width] = hand[j]
+    for j in range(share):
+        hand_over(j, j).wait_send()
+
+
+def fused_shards(
+    group_in, w_qkv, w_out, step_sizes, fast_weights, momentum, momentum_decay, fast_rate
+):
+    sections, n = lax.axis_size("section"), lax.axis_size("tok")
+    tokens = group_in[0]
+    rows = tokens.shape[0]
+    heads, fin, hid = fast_weights.shape[1], fast_weights.shape[3], fast_weights.shape[4]
+    local, width = heads * fin, w_qkv.shape[2]
+    all_rows, share = rows * n, n // 2
+    chunks, qchunks = all_rows // CHUNK, all_rows // QUERY_CHUNK
+    matrices = heads * 3
+    rate_lines = jnp.pad(step_sizes[0].T, ((0, 8 - heads), (0, 0)))
+    vmem = pl.BlockSpec(memory_space=pltpu.VMEM)
+    smem = pl.BlockSpec(memory_space=pltpu.SMEM)
+    anywhere = pl.BlockSpec(memory_space=pl.ANY)
+    dma = pltpu.SemaphoreType.DMA
+    handed, updated = pl.pallas_call(
+        functools.partial(layer_kernel, (sections, n, heads, fin, hid)),
+        out_shape=(
+            jax.ShapeDtypeStruct((rows, share * width), BF16),
+            jax.ShapeDtypeStruct((matrices, fin, hid), BF16),
+        ),
+        in_specs=[vmem, vmem, smem, smem, anywhere, anywhere, anywhere, anywhere],
+        out_specs=(vmem, anywhere),
+        scratch_shapes=[
+            pltpu.VMEM(w_qkv.shape[1:], BF16),
+            pltpu.VMEM(w_out.shape[1:], BF16),
+            pltpu.VMEM((matrices, fin, hid), BF16),
+            pltpu.VMEM((matrices, fin, hid), BF16),
+            pltpu.VMEM((fin, hid), BF16),
+            pltpu.VMEM((n, 2, rows // 2, width), BF16),
+            pltpu.VMEM((heads, n, rows, rows), F32),
+            pltpu.VMEM((n, 8, rows), F32),
+            pltpu.VMEM((chunks, CHUNK, 2 * local), BF16),
+            pltpu.VMEM((chunks, CHUNK, 2 * local), BF16),
+            pltpu.VMEM((chunks, CHUNK, 2 * local), BF16),
+            pltpu.VMEM((chunks, CHUNK, 2 * local), BF16),
+            pltpu.VMEM((qchunks, QUERY_CHUNK, local), BF16),
+            pltpu.VMEM((qchunks, QUERY_CHUNK, local), BF16),
+            pltpu.VMEM((qchunks, QUERY_CHUNK, local), BF16),
+            pltpu.VMEM((qchunks, QUERY_CHUNK, local), BF16),
+            pltpu.VMEM((3, fin, hid), F32),
+            pltpu.VMEM((matrices, fin, hid), BF16),
+            pltpu.VMEM((all_rows, local), BF16),
+            pltpu.VMEM((all_rows // 2, width), BF16),
+            pltpu.VMEM((all_rows // 2, width), BF16),
+            pltpu.VMEM((share, rows, width), BF16),
+            pltpu.VMEM((share, rows, width), BF16),
+            dma((4,)),
+            dma((n,)), dma((n,)), dma((n,)), dma((n,)), dma((n,)), dma((n,)),
+            dma((chunks,)), dma((chunks,)), dma((chunks,)), dma((chunks,)), dma((chunks,)),
+            dma((qchunks,)), dma((qchunks,)), dma((qchunks,)), dma((qchunks,)), dma((qchunks,)),
+            dma((matrices,)), dma(()), dma(()), dma((share,)), dma((share,)),
+        ],
+        compiler_params=pltpu.CompilerParams(
+            collective_id=0, has_side_effects=True, vmem_limit_bytes=60 << 20
+        ),
+    )(
+        tokens, rate_lines, momentum_decay[0], fast_rate[0], w_qkv[0], w_out[0],
+        fast_weights[0].reshape(matrices, fin, hid), momentum[0].reshape(matrices, fin, hid),
+    )
+    return (handed[None], updated.reshape(fast_weights.shape))
+
+
+def shards(group_in, w_qkv, w_out, *rest):
+    n, cores = lax.axis_size("tok"), lax.axis_size("head")
+    rows, width, local = group_in.shape[1], w_qkv.shape[2], w_qkv.shape[3]
+    held = 2 * (24 * rows * n * local + 12 * rows * n * width + 4 * w_qkv[0].size)
+    fits = (
+        held < 44 << 20
+        and cores == 2
+        and n % 2 == 0
+        and n >= 4
+        and rows == 128
+        and width % 128 == 0
+        and w_out.shape[2] == width
+        and lax.axis_size("section") > 2
+    )
+    return (fused_shards if fits else plain_shards)(group_in, w_qkv, w_out, *rest)
+
+
 def solution(mesh):
     placed = (
         P("section", "tok", None),

time: 257 us -> 202 us (0.79)
  Pallas kernels: 0 us -> 195 us
  waiting for transfers between devices: 112 us -> 0 us
  blocking collectives: 43.3 us -> 0 us
  matrix products: 37.3 us -> 0 us
  other arithmetic: 26.1 us -> 0 us
  between operations: 14.3 us -> 0.64 us
  local copies, waits for them, and re-layouts: 20 us -> 6.89 us
    pallas_call x0 -> x1, Pallas kernels: none -> 195 us  [fused_shards(): pl.pallas_call(functools.partial(layer_kernel, (sections, n, heads, fin,...]
    psum x1 -> x0, waiting for transfers between devices: 103 us -> none  [shards(): summed_kv = lax.psum(partial_kv, 'tok').astype(jnp.float32)]
    dot_general x17 -> x0, matrix products: 37.3 us -> none  [the longest x2 9.3 us: newton_step(): jnp.einsum('mij,mjk->mik', cubic_term.astype(jnp.bfloat16), gram_matrix,...]
    all_to_all x2 -> x0, blocking collectives: 35.3 us -> none  [the longest x1 19.2 us: shards(): lax.all_to_all(tokens, 'tok', split_axis=1, concat_axis=0, tiled=True)]
    convert_element_type x5 -> x0, other arithmetic: 22.5 us -> none  [the longest x2 11.5 us: shards(): updated = (fast_weights[0].astype(jnp.float32) - fast_rate[0][:, None, No...]
    reduce_scatter x1 -> x0, waiting for transfers between devices: 8.58 us -> none  [shards(): lax.psum_scatter(own_rows, 'head', scatter_dimension=1, tiled=True)]
    all_gather x1 -> x0, blocking collectives: 8.08 us -> none  [shards(): rates = lax.all_gather(step_sizes[0], 'tok', axis=0, tiled=True)]
    convert_element_type x1 -> x0, local copies, waits for them, and re-layouts: 3.36 us -> none  [shards(): moment = decay_rate * momentum[0].astype(jnp.float32) + summed]
  transfers between devices with their start and end apart: 3 -> 0, of which waited for: 3 -> 0; matrix products, arithmetic and copies ran while one was open for 7% -> 0% of each run, Pallas kernels for 0% -> 0%
where the time goes in v2:
time: 202 us
  Pallas kernels  195 us (97%)
  local copies, waits for them, and re-layouts  6.89 us (3%)
    pallas_call x1, Pallas kernels, fused_shards(): pl.pallas_call(functools.partial(layer_kernel, (sections, n, heads, fin,...  195 us
    unnamed x2, local copies, waits for them, and re-layouts  5.61 us

profile of v2, /device:TPU:1, one launch (start us, length us, event | category | flops | bytes accessed | tf_op | source)
XLA Modules:
  0.0 202.1 jit_solution(3042828320667027120)
XLA Ops:
  0.6 1.3 pad.4.rate_ref
  1.9 194.5 %shard_map.95 = (bf16[128,1024]{1,0:T(8,128)(2,1)}, bf16[6,512,512]{2,1,0:T(8,128)(2,1)}) custom-call(bf16[128,2048]{1,0:T(8,128)(2,1)} %bitcast.17, f32[8,128]{1,0:T(8,128)} %pad.4.rate_ref, f32[2]{0:T(128)} %bitcast.20, f32[2]{0:T(128)} %bitcast.21, bf16[3,512,1024]{2,1,0:T(8,128)(2,1)} %bitcast.13, bf16[1024,512]{1,0:T(8,128)(2,1)} %bitcast.16, ...), custom_call_target="tpu_custom_call" | custom-call | tf_op jit(solution)/shard_map/pallas_call | solution.py:483
  196.5 1.7 copy.12
  198.1 3.9 %copy.13 = bf16[1,2,3,512,512]{4,3,2,1,0:T(8,128)(2,1)} copy(bf16[1,2,3,512,512]{4,3,2,1,0:T(8,128)(2,1)} %bitcast.12) | data formatting | bytes 6291456

commit v3 on v2

--- a/solution.py
+++ b/solution.py
@@ -135,6 +135,7 @@
 BF16 = jnp.bfloat16
 CHUNK = 32
 QUERY_CHUNK = 64
+LAG = 3
 
 
 def dot(a, b, a_dim=1, b_dim=0):
@@ -332,9 +333,9 @@
         def _(c):
             gather(c)
 
-            @pl.when(c >= 2)
-            def _():
-                spread(c - 2)
+            @pl.when(jnp.logical_not(is_end) & (c >= LAG))
+            def _():
+                spread(c - LAG)
 
     tile = columns[...].reshape(all_rows, width)
     qpart[...] = dot(tile, wqkv[0]).astype(BF16).reshape(qchunks, QUERY_CHUNK, local)
@@ -345,8 +346,15 @@
         def _(c):
             qgather(c)
 
-    spread(chunks - 2)
-    spread(chunks - 1)
+        @pl.loop(0, chunks)
+        def _(c):
+            spread(c)
+
+    @pl.when(jnp.logical_not(is_end))
+    def _():
+        @pl.loop(chunks - LAG, chunks)
+        def _(c):
+            spread(c)
 
     def query_step(c):
         @pl.when(jnp.logical_not(is_end) & (c < qchunks))

time: 202 us -> 126 us (0.62)
  Pallas kernels: 195 us -> 118 us
    pallas_call x1, Pallas kernels: 195 us -> 118 us  [fused_shards(): pl.pallas_call(functools.partial(layer_kernel, (sections, n, heads, fin,...]
where the time goes in v3:
time: 126 us; the launch traced here: 125 us
  Pallas kernels  118 us (94%)
  local copies, waits for them, and re-layouts  6.89 us (5%)
    pallas_call x1, Pallas kernels, fused_shards(): pl.pallas_call(functools.partial(layer_kernel, (sections, n, heads, fin,...  118 us
    unnamed x2, local copies, waits for them, and re-layouts  5.61 us

profile of v3, /device:TPU:1, one launch (start us, length us, event | category | flops | bytes accessed | tf_op | source)
XLA Modules:
  0.0 125.3 jit_solution(6709959729283505254)
XLA Ops:
  0.6 1.3 %pad.4.rate_ref = f32[8,128]{1,0:T(8,128)} pad(f32[2,128]{1,0:T(2,128)} %bitcast.19, f32[]{:T(128)} %constant.2.clone.1), padding=0_6x0_0 | pad | bytes 5124 | tf_op jit(solution)/shard_map/jit(_pad)/pad | solution.py:486
  1.9 117.8 %shard_map.95 = (bf16[128,1024]{1,0:T(8,128)(2,1)}, bf16[6,512,512]{2,1,0:T(8,128)(2,1)}) custom-call(bf16[128,2048]{1,0:T(8,128)(2,1)} %bitcast.17, f32[8,128]{1,0:T(8,128)} %pad.4.rate_ref, f32[2]{0:T(128)} %bitcast.20, f32[2]{0:T(128)} %bitcast.21, bf16[3,512,1024]{2,1,0:T(8,128)(2,1)} %bitcast.13, bf16[1024,512]{1,0:T(8,128)(2,1)} %bitcast.16, ...), custom_call_target="tpu_custom_call" | custom-call | tf_op jit(solution)/shard_map/pallas_call | solution.py:491
  119.7 1.7 %copy.12 = bf16[1,128,1024]{2,1,0:T(8,128)(2,1)} copy(bf16[1,128,1024]{2,1,0:T(8,128)(2,1)} %bitcast.18) | data formatting | bytes 524288
  121.4 3.9 %copy.13 = bf16[1,2,3,512,512]{4,3,2,1,0:T(8,128)(2,1)} copy(bf16[1,2,3,512,512]{4,3,2,1,0:T(8,128)(2,1)} %bitcast.12) | data formatting | bytes 6291456

commit v4 on v3

--- a/solution.py
+++ b/solution.py
@@ -176,8 +176,7 @@
             [(wqkv_hbm, wqkv), (fast_hbm, fast), (mom_hbm, mom), (wout_hbm, wout)]
         )
     ]
-    for load in loads:
-        load.start()
+    loads[0].start()
 
     barrier = pltpu.get_barrier_semaphore()
 
@@ -324,6 +323,8 @@
 
         if block == 0:
             loads[0].wait()
+            for load in loads[1:]:
+                load.start()
         tile = columns[block].reshape(rows, width)
         for j in range(2):
             made = dot(tile, wqkv[j + 1]).astype(BF16).reshape(per_block, CHUNK, local)
@@ -337,8 +338,11 @@
             def _():
                 spread(c - LAG)
 
-    tile = columns[...].reshape(all_rows, width)
-    qpart[...] = dot(tile, wqkv[0]).astype(BF16).reshape(qchunks, QUERY_CHUNK, local)
+        made = dot(columns[block].reshape(rows, width), wqkv[0]).astype(BF16)
+        per_query = rows // QUERY_CHUNK
+        qpart[block * per_query : (block + 1) * per_query] = made.reshape(
+            per_query, QUERY_CHUNK, local
+        )
 
     @pl.when(is_end)
     def _():
@@ -361,9 +365,9 @@
         def _():
             qgather(c)
 
-        @pl.when(jnp.logical_not(is_end) & (c >= 2) & (c < qchunks + 2))
+        @pl.when(jnp.logical_not(is_end) & (c >= LAG) & (c < qchunks + LAG))
         def _():
-            qspread(c - 2)
+            qspread(c - LAG)
 
     loads[1].wait()
     loads[2].wait()
@@ -406,9 +410,10 @@
                 fast[m].astype(F32) - fast_rate_ref[h] * moved[...].astype(F32)
             ).astype(BF16)
             store_next(m).start()
-            query_step(m)
-
-    @pl.loop(heads * 3, qchunks + 2)
+            query_step(2 * m)
+            query_step(2 * m + 1)
+
+    @pl.loop(heads * 6, max(heads * 6, qchunks + LAG))
     def _(c):
         query_step(c)
 

time: 126 us -> 125 us (level)
  no operation moved by 1% of the time
where the time goes in v4:
time: 125 us
  Pallas kernels  117 us (94%)
  local copies, waits for them, and re-layouts  6.89 us (6%)
    pallas_call x1, Pallas kernels, fused_shards(): pl.pallas_call(functools.partial(layer_kernel, (sections, n, heads, fin,...  117 us
    unnamed x2, local copies, waits for them, and re-layouts  5.61 us

profile of v4, /device:TPU:1, one launch (start us, length us, event | category | flops | bytes accessed | tf_op | source)
XLA Modules:
  0.0 124.8 jit_solution(1253019869346293342)
XLA Ops:
  0.6 1.3 %pad.4.rate_ref = f32[8,128]{1,0:T(8,128)} pad(f32[2,128]{1,0:T(2,128)} %bitcast.19, f32[]{:T(128)} %constant.2.clone.1), padding=0_6x0_0 | pad | bytes 5124 | tf_op jit(solution)/shard_map/jit(_pad)/pad | solution.py:491
  1.9 117.3 %shard_map.95 = (bf16[128,1024]{1,0:T(8,128)(2,1)}, bf16[6,512,512]{2,1,0:T(8,128)(2,1)}) custom-call(bf16[128,2048]{1,0:T(8,128)(2,1)} %bitcast.17, f32[8,128]{1,0:T(8,128)} %pad.4.rate_ref, f32[2]{0:T(128)} %bitcast.20, f32[2]{0:T(128)} %bitcast.21, bf16[3,512,1024]{2,1,0:T(8,128)(2,1)} %bitcast.13, bf16[1024,512]{1,0:T(8,128)(2,1)} %bitcast.16, ...), custom_call_target="tpu_custom_call" | custom-call | tf_op jit(solution)/shard_map/pallas_call | solution.py:496
  119.2 1.7 %copy.12 = bf16[1,128,1024]{2,1,0:T(8,128)(2,1)} copy(bf16[1,128,1024]{2,1,0:T(8,128)(2,1)} %bitcast.18) | data formatting | bytes 524288
  120.9 3.9 %copy.13 = bf16[1,2,3,512,512]{4,3,2,1,0:T(8,128)(2,1)} copy(bf16[1,2,3,512,512]{4,3,2,1,0:T(8,128)(2,1)} %bitcast.12) | data formatting | bytes 6291456
